TPU v7x, 128 devices: a whole 4x4x4 slice. The times are simulated.
128 devices in a mesh: pair: 8 (over x, core), ints: 16 (over y, z).
Axes of the slice: x: 4, y: 4, z: 4, core: 2. Of those that a mesh axis runs over, the one named last changes fastest.
Arguments:
- t2: bfloat16 [4096, 8192], P('pair', 'ints'), may hold values from -6 to 6
- t2_live: int32 [8, 64], P('pair', 'ints'), may hold values 0 or 1
- int_tiles: int32 [5120, 2], P('ints'), may hold values from 0 to 63
- integrals: bfloat16 [5120, 128, 128], P('ints'), may hold values from -0.0625 to 0.0625
- cycle_w: bfloat16 [4096, 4096], P('pair'), may hold values from -0.09375 to 0.09375
- res_live: int32 [8, 64], P('pair', 'ints'), may hold values 0 or 1
Outputs:
- residual: float32 [4096, 8192], P('pair', 'ints')
All inputs are finite; a program needn't handle non-finite values. No bound on the sum of `t2_live` or of `res_live` on one device may be relied on, other than what follows from the above.
Results may differ from a plain program's by a relative error of at most 0.0003.
Values may be sent and summed in bfloat16 or wider, within the bound.
No kernel may reach another device: no remote copies, remote signals or barrier semaphores. Data moves between devices by JAX's collectives and lax.ppermute only.
A program may use at most 192 MiB of HBM per device.

v0:
```python
import jax
import jax.numpy as jnp
from jax import lax
from jax.sharding import PartitionSpec as P


def local(t2, t2_live, int_tiles, integrals, cycle_w, res_live):
    rows_here = t2.shape[0]
    tile_size = integrals.shape[1]
    tiles_here = t2.shape[1] // tile_size
    live_mask = t2_live[0].astype(t2.dtype)
    amps = (t2.reshape(rows_here, tiles_here, tile_size) * live_mask[None, :, None]).reshape(
        rows_here, tiles_here * tile_size
    )
    block_amps = lax.all_gather(amps, "ints", axis=1, tiled=True)
    tiles_all = block_amps.shape[1] // tile_size
    amps_tiled = block_amps.reshape(rows_here, tiles_all, tile_size)
    count_here = integrals.shape[0]
    group_size = 64
    tile_groups = int_tiles.reshape(count_here // group_size, group_size, 2)
    int_groups = integrals.reshape(count_here // group_size, group_size, tile_size, tile_size)
    tile_ids = jnp.arange(tiles_all, dtype=jnp.int32)

    def ladder_step(partial_value, entry):
        pairs_uv, blocks = entry
        source_table = (pairs_uv[:, 0:1] == tile_ids[None, :]).astype(jnp.bfloat16)
        target_table = (pairs_uv[:, 1:2] == tile_ids[None, :]).astype(jnp.float32)
        picked = jnp.einsum(
            "jt,ptc->jpc", source_table, amps_tiled, preferred_element_type=jnp.float32
        ).astype(jnp.bfloat16)
        product = jnp.einsum("jpc,jcd->jpd", picked, blocks, preferred_element_type=jnp.float32)
        partial_value = partial_value + jnp.einsum(
            "jv,jpd->vpd", target_table, product, precision=lax.Precision.HIGHEST
        )
        return (partial_value, None)

    start_sum = jnp.zeros((tiles_all, rows_here, tile_size), jnp.float32)
    partial_value, _ = lax.scan(ladder_step, start_sum, (tile_groups, int_groups))
    summed = lax.psum(partial_value, "ints")
    owned = lax.dynamic_slice_in_dim(summed, lax.axis_index("ints") * tiles_here, tiles_here, 0)
    ladder = owned.transpose(1, 0, 2).reshape(rows_here, tiles_here * tile_size)
    cycle_term = jnp.dot(
        cycle_w,
        lax.all_gather(amps, "pair", axis=0, tiled=True),
        preferred_element_type=jnp.float32,
    )
    keep_mask = jnp.repeat(res_live[0], tile_size).astype(jnp.float32)[None, :]
    return keep_mask * (ladder + cycle_term)


def solution(mesh):
    placed = (
        P("pair", "ints"),
        P("pair", "ints"),
        P("ints", None),
        P("ints", None, None),
        P("pair", None),
        P("pair", "ints"),
    )
    return jax.shard_map(
        local, mesh=mesh, in_specs=placed, out_specs=P("pair", "ints"), check_vma=False
    )
```

profile of v0, /device:TPU:1, one launch (start us, length us, event | category | flops | bytes accessed | tf_op | source)
XLA Modules:
  0.0 551.5 jit_solution(12331240370962497261)
XLA Ops:
  7.4 0.7 convert_bitcast_fusion
  8.0 0.1 broadcast_bitcast_fusion.1
  8.1 1.9 broadcast_multiply_fusion
  10.0 0.0 all-reduce.2.cloned.1.call-start
  10.1 0.8 reshape.30
  10.8 80.4 %all-gather.3.cloned.1.call-done = bf16[512,8192]{1,0:T(8,128)(2,1)} async-done(((bf16[512,512]{1,0:T(8,128)(2,1)}), bf16[512,8192]{1,0:T(8,128)(2,1)}) %all-gather.3.cloned.1.call-update) | async-done | bytes 8388624 | tf_op jit(solution)/shard_map/all_gather | solution.py:15
  91.2 9.3 %copy.15 = bf16[64,8,64,128]{3,2,1,0:T(8,128)(2,1)} copy(bf16[64,8,64,128]{3,1,2,0:T(8,128)(2,1)} %bitcast.55) | data formatting | bytes 16777216
  100.5 213.6 %while.12 = (s32[]{:T(128)}, f32[64,512,128]{2,0,1:T(8,128)}, s32[5,64,2]{1,0,2:T(8,128)S(1)}, bf16[512,64,128]{2,1,0:T(8,128)(2,1)}, bf16[5,64,128,128]{3,2,1,0:T(8,128)(2,1)}, /*index=5*/s32[]{:T(128)}, s32[]{:T(128)}) while((s32[]{:T(128)}, f32[64,512,128]{2,0,1:T(8,128)}, s32[5,64,2]{1,0,2:T(8,128)S(1)}, ...), condition=%wide.region_1.2_spmd.clone.clone, body=%wide.region_0.1_spmd.clone.clone.sunk | while | flops 4840235008 | bytes 94374496 | solution.py:38
  100.5 5.8 %fusion.34 = bf16[64,512,128]{2,0,1:T(8,128)(2,1)S(1)} fusion(bf16[512,64,128]{2,1,0:T(8,128)(2,1)} %get-tuple-element.146, s32[64]{0:T(128)S(1)} %get-tuple-element.127), kind=kOutput, calls=%fused_computation.12.clone.1 | convolution fusion | flops 536875008 | bytes 16777472 | tf_op jit(solution)/shard_map/while/body/eval_jaxpr/jt,ptc->jpc/dot_general | solution.py:28
  106.3 13.9 %fusion.35 = f32[64,512,128]{2,1,0:T(8,128)} fusion(bf16[64,512,128]{2,0,1:T(8,128)(2,1)S(1)} %fusion.34, bf16[5,64,128,128]{3,2,1,0:T(8,128)(2,1)} %get-tuple-element.147, s32[]{:T(128)S(6)} %copy.28), kind=kOutput, calls=%fused_computation.5.clone.1 | convolution fusion | flops 1073741824 | bytes 27262980 | tf_op jit(solution)/shard_map/while/body/eval_jaxpr/jpc,jcd->jpd/dot_general | solution.py:31
  120.2 20.4 %select_add_fusion.2 = f32[64,512,128]{2,0,1:T(8,128)} fusion(f32[64,512,128]{2,0,1:T(8,128)} %get-tuple-element.137, f32[64,512,128]{2,1,0:T(8,128)} %fusion.35, pred[]{:T(512)S(6)} %compare.3, s32[64]{0:T(128)S(1)} %get-tuple-element.128), kind=kOutput, calls=%fused_computation.4.clone.1 | convolution fusion | flops 3229618176 | bytes 50331904 | tf_op jit(solution)/shard_map/while/body/eval_jaxpr/jv,jpd->vpd/dot_general | solution.py:32
  140.6 5.8 %fusion.34 = bf16[64,512,128]{2,0,1:T(8,128)(2,1)S(1)} fusion(bf16[512,64,128]{2,1,0:T(8,128)(2,1)} %get-tuple-element.146, s32[64]{0:T(128)S(1)} %get-tuple-element.127), kind=kOutput, calls=%fused_computation.12.clone.1 | convolution fusion | flops 536875008 | bytes 16777472 | tf_op jit(solution)/shard_map/while/body/eval_jaxpr/jt,ptc->jpc/dot_general | solution.py:28
  146.4 13.9 %fusion.35 = f32[64,512,128]{2,1,0:T(8,128)} fusion(bf16[64,512,128]{2,0,1:T(8,128)(2,1)S(1)} %fusion.34, bf16[5,64,128,128]{3,2,1,0:T(8,128)(2,1)} %get-tuple-element.147, s32[]{:T(128)S(6)} %copy.28), kind=kOutput, calls=%fused_computation.5.clone.1 | convolution fusion | flops 1073741824 | bytes 27262980 | tf_op jit(solution)/shard_map/while/body/eval_jaxpr/jpc,jcd->jpd/dot_general | solution.py:31
  160.3 23.7 %select_add_fusion.2 = f32[64,512,128]{2,0,1:T(8,128)} fusion(f32[64,512,128]{2,0,1:T(8,128)} %get-tuple-element.137, f32[64,512,128]{2,1,0:T(8,128)} %fusion.35, pred[]{:T(512)S(6)} %compare.3, s32[64]{0:T(128)S(1)} %get-tuple-element.128), kind=kOutput, calls=%fused_computation.4.clone.1 | convolution fusion | flops 3229618176 | bytes 50331904 | tf_op jit(solution)/shard_map/while/body/eval_jaxpr/jv,jpd->vpd/dot_general | solution.py:32
  184.0 5.8 %fusion.34 = bf16[64,512,128]{2,0,1:T(8,128)(2,1)S(1)} fusion(bf16[512,64,128]{2,1,0:T(8,128)(2,1)} %get-tuple-element.146, s32[64]{0:T(128)S(1)} %get-tuple-element.127), kind=kOutput, calls=%fused_computation.12.clone.1 | convolution fusion | flops 536875008 | bytes 16777472 | tf_op jit(solution)/shard_map/while/body/eval_jaxpr/jt,ptc->jpc/dot_general | solution.py:28
  189.8 13.9 %fusion.35 = f32[64,512,128]{2,1,0:T(8,128)} fusion(bf16[64,512,128]{2,0,1:T(8,128)(2,1)S(1)} %fusion.34, bf16[5,64,128,128]{3,2,1,0:T(8,128)(2,1)} %get-tuple-element.147, s32[]{:T(128)S(6)} %copy.28), kind=kOutput, calls=%fused_computation.5.clone.1 | convolution fusion | flops 1073741824 | bytes 27262980 | tf_op jit(solution)/shard_map/while/body/eval_jaxpr/jpc,jcd->jpd/dot_general | solution.py:31
  203.7 23.7 %select_add_fusion.2 = f32[64,512,128]{2,0,1:T(8,128)} fusion(f32[64,512,128]{2,0,1:T(8,128)} %get-tuple-element.137, f32[64,512,128]{2,1,0:T(8,128)} %fusion.35, pred[]{:T(512)S(6)} %compare.3, s32[64]{0:T(128)S(1)} %get-tuple-element.128), kind=kOutput, calls=%fused_computation.4.clone.1 | convolution fusion | flops 3229618176 | bytes 50331904 | tf_op jit(solution)/shard_map/while/body/eval_jaxpr/jv,jpd->vpd/dot_general | solution.py:32
  227.4 5.8 %fusion.34 = bf16[64,512,128]{2,0,1:T(8,128)(2,1)S(1)} fusion(bf16[512,64,128]{2,1,0:T(8,128)(2,1)} %get-tuple-element.146, s32[64]{0:T(128)S(1)} %get-tuple-element.127), kind=kOutput, calls=%fused_computation.12.clone.1 | convolution fusion | flops 536875008 | bytes 16777472 | tf_op jit(solution)/shard_map/while/body/eval_jaxpr/jt,ptc->jpc/dot_general | solution.py:28
  233.1 13.9 %fusion.35 = f32[64,512,128]{2,1,0:T(8,128)} fusion(bf16[64,512,128]{2,0,1:T(8,128)(2,1)S(1)} %fusion.34, bf16[5,64,128,128]{3,2,1,0:T(8,128)(2,1)} %get-tuple-element.147, s32[]{:T(128)S(6)} %copy.28), kind=kOutput, calls=%fused_computation.5.clone.1 | convolution fusion | flops 1073741824 | bytes 27262980 | tf_op jit(solution)/shard_map/while/body/eval_jaxpr/jpc,jcd->jpd/dot_general | solution.py:31
  247.1 23.7 %select_add_fusion.2 = f32[64,512,128]{2,0,1:T(8,128)} fusion(f32[64,512,128]{2,0,1:T(8,128)} %get-tuple-element.137, f32[64,512,128]{2,1,0:T(8,128)} %fusion.35, pred[]{:T(512)S(6)} %compare.3, s32[64]{0:T(128)S(1)} %get-tuple-element.128), kind=kOutput, calls=%fused_computation.4.clone.1 | convolution fusion | flops 3229618176 | bytes 50331904 | tf_op jit(solution)/shard_map/while/body/eval_jaxpr/jv,jpd->vpd/dot_general | solution.py:32
  270.7 5.8 %fusion.34 = bf16[64,512,128]{2,0,1:T(8,128)(2,1)S(1)} fusion(bf16[512,64,128]{2,1,0:T(8,128)(2,1)} %get-tuple-element.146, s32[64]{0:T(128)S(1)} %get-tuple-element.127), kind=kOutput, calls=%fused_computation.12.clone.1 | convolution fusion | flops 536875008 | bytes 16777472 | tf_op jit(solution)/shard_map/while/body/eval_jaxpr/jt,ptc->jpc/dot_general | solution.py:28
  276.5 13.9 %fusion.35 = f32[64,512,128]{2,1,0:T(8,128)} fusion(bf16[64,512,128]{2,0,1:T(8,128)(2,1)S(1)} %fusion.34, bf16[5,64,128,128]{3,2,1,0:T(8,128)(2,1)} %get-tuple-element.147, s32[]{:T(128)S(6)} %copy.28), kind=kOutput, calls=%fused_computation.5.clone.1 | convolution fusion | flops 1073741824 | bytes 27262980 | tf_op jit(solution)/shard_map/while/body/eval_jaxpr/jpc,jcd->jpd/dot_general | solution.py:31
  290.4 23.7 %select_add_fusion.2 = f32[64,512,128]{2,0,1:T(8,128)} fusion(f32[64,512,128]{2,0,1:T(8,128)} %get-tuple-element.137, f32[64,512,128]{2,1,0:T(8,128)} %fusion.35, pred[]{:T(512)S(6)} %compare.3, s32[64]{0:T(128)S(1)} %get-tuple-element.128), kind=kOutput, calls=%fused_computation.4.clone.1 | convolution fusion | flops 3229618176 | bytes 50331904 | tf_op jit(solution)/shard_map/while/body/eval_jaxpr/jv,jpd->vpd/dot_general | solution.py:32
  314.1 0.2 all-gather.5.cloned.1.call-start
  314.4 0.3 all-gather.5.cloned.1.call-update
  314.7 0.0 copy-done
  314.8 0.1 broadcast_bitcast_fusion
  314.8 219.9 %all-reduce.2.cloned.1.call-done = f32[64,512,128]{2,0,1:T(8,128)} async-done(((f32[64,512,128]{2,0,1:T(8,128)}), f32[64,512,128]{2,0,1:T(8,128)}) %all-reduce.2.cloned.1.call-update) | async-done | bytes 16777232 | tf_op jit(solution)/shard_map/psum | solution.py:39
  534.7 1.8 dynamic-slice_bitcast_fusion
  536.5 0.4 copy.10
  536.9 5.8 %fusion.18 = f32[512,512]{0,1:T(8,128)S(1)} fusion(f32[512,512]{0,1:T(8,128)S(1)} %bitcast.56, bf16[4096,512]{1,0:T(8,128)(2,1)} %all-gather.5.cloned.1.call-done, bf16[512,4096]{1,0:T(8,128)(2,1)} %param.12, f32[512]{0:T(512)S(1)} %broadcast_bitcast_fusion), kind=kOutput, calls=%fused_computation.21 | convolution fusion | flops 2148007936 | bytes 10487808 | tf_op jit(solution)/shard_map/dot_general | solution.py:42
  542.8 1.3 copy.11
  (17 shorter events, 0.1 us)
Async XLA Ops:
  7.4 83.8 %all-gather.3.cloned.1.call-start = ((), (), s32[]{:S(2)}) async-start(), calls=%async_computation | async-start | bytes 8912896 | tf_op jit(solution)/shard_map/all_gather | solution.py:15
  10.0 524.7 %all-reduce.2.cloned.1.call-start = ((), (), s32[]{:S(2)}) async-start(), calls=%async_computation.1 | async-start | bytes 33554432 | tf_op jit(solution)/shard_map/psum | solution.py:39
  314.1 0.7 copy-start
  314.1 222.8 %all-gather.5.cloned.1.call-start = ((), (), s32[]{:S(2)}) async-start(), calls=%async_computation.2 | async-start | bytes 4718592 | tf_op jit(solution)/shard_map/all_gather | solution.py:44
Sparse Core Ops, SparseCore 0:
  10.3 80.8 all-gather.2
  314.2 220.4 all-reduce.1
Sparse Core Ops, SparseCore 1:
  316.3 32.4 all-gather.4
where the time goes:
time: 552 us
  waiting for transfers between devices  301 us (55%)
  matrix products  219 us (40%)
  between operations  14.9 us (3%)
  local copies, waits for them, and re-layouts  13.7 us (2%)
    psum x1, waiting for transfers between devices, local(): summed = lax.psum(partial_value, 'ints')  220 us
    dot_general x5, matrix products, ladder_step(): jnp.einsum('jv,jpd->vpd', target_table, product, precision=lax.Precision....  115 us
    all_gather x1, waiting for transfers between devices, local(): block_amps = lax.all_gather(amps, 'ints', axis=1, tiled=True)  80.4 us
    dot_general x5, matrix products, ladder_step(): jnp.einsum('jpc,jcd->jpd', picked, blocks, preferred_element_type=jnp.flo...  69.7 us
    dot_general x5, matrix products, ladder_step(): jnp.einsum('jt,ptc->jpc', source_table, amps_tiled, preferred_element_typ...  28.8 us
  transfers between devices with their start and end apart: 3, of which 2 were waited for; matrix products, arithmetic and copies ran while one was open for 1% of the time, Pallas kernels for 0%

commit v1 on v0

--- a/solution.py
+++ b/solution.py
@@ -12,7 +12,9 @@
     amps = (t2.reshape(rows_here, tiles_here, tile_size) * live_mask[None, :, None]).reshape(
         rows_here, tiles_here * tile_size
     )
-    block_amps = lax.all_gather(amps, "ints", axis=1, tiled=True)
+    w2 = tuple((amps for _ in range(lax.axis_size("ints"))))
+    built = lax.all_to_all(jnp.stack(w2, 0), axis_name="ints", split_axis=0, concat_axis=0)
+    block_amps = jnp.concatenate(built, 1)
     tiles_all = block_amps.shape[1] // tile_size
     amps_tiled = block_amps.reshape(rows_here, tiles_all, tile_size)
     count_here = integrals.shape[0]

time: 552 us -> 649 us (1.18)
  waiting for transfers between devices: 301 us -> 371 us
  local copies, waits for them, and re-layouts: 13.7 us -> 32.2 us
  starting transfers between devices: 0.27 us -> 9.05 us
    all_to_all x0 -> x1, waiting for transfers between devices: none -> 146 us  [local(): lax.all_to_all(jnp.stack(w2, 0), axis_name='ints', split_axis=0, concat_a...]
    all_gather x1 -> x0, waiting for transfers between devices: 80.4 us -> none  [local(): block_amps = lax.all_gather(amps, 'ints', axis=1, tiled=True)]
    all_to_all x0 -> x1, local copies, waits for them, and re-layouts: none -> 12.3 us  [local(): lax.all_to_all(jnp.stack(w2, 0), axis_name='ints', split_axis=0, concat_a...]
    all_to_all x0 -> x1, starting transfers between devices: none -> 8.78 us  [local(): lax.all_to_all(jnp.stack(w2, 0), axis_name='ints', split_axis=0, concat_a...]
  transfers between devices with their start and end apart: 3 -> 3, of which waited for: 2 -> 2; matrix products, arithmetic and copies ran while one was open for 1% -> 0% of each run, Pallas kernels for 0% -> 0%
where the time goes in v1:
time: 649 us; the launch traced here: 648 us
  waiting for transfers between devices  371 us (57%)
  matrix products  220 us (34%)
  local copies, waits for them, and re-layouts  32.2 us (5%)
  between operations  14.9 us (2%)
  starting transfers between devices  9.05 us (1%)
    psum x1, waiting for transfers between devices, local(): summed = lax.psum(partial_value, 'ints')  224 us
    all_to_all x1, waiting for transfers between devices, local(): lax.all_to_all(jnp.stack(w2, 0), axis_name='ints', split_axis=0, concat_a...  146 us
    dot_general x5, matrix products, ladder_step(): jnp.einsum('jv,jpd->vpd', target_table, product, precision=lax.Precision....  115 us
    dot_general x5, matrix products, ladder_step(): jnp.einsum('jpc,jcd->jpd', picked, blocks, preferred_element_type=jnp.flo...  69.9 us
    dot_general x5, matrix products, ladder_step(): jnp.einsum('jt,ptc->jpc', source_table, amps_tiled, preferred_element_typ...  28.8 us
  transfers between devices with their start and end apart: 3, of which 2 were waited for; matrix products, arithmetic and copies ran while one was open for 0% of the time, Pallas kernels for 0%

profile of v1, /device:TPU:1, one launch (start us, length us, event | category | flops | bytes accessed | tf_op | source)
XLA Modules:
  0.0 648.3 jit_solution(3241296732083674341)
XLA Ops:
  7.4 0.7 convert_bitcast_fusion
  8.0 0.1 broadcast_bitcast_fusion.1
  8.1 1.1 broadcast_multiply_fusion
  9.2 4.0 stack.3
  13.2 8.8 %all-to-all-start = ((bf16[16,512,512]{2,1,0:T(8,128)(2,1)}), bf16[16,512,512]{2,1,0:T(8,128)(2,1)}, u32[]{:S(2)}, u32[]{:S(2)}) async-start(bf16[16,512,512]{2,1,0:T(8,128)(2,1)} %stack.3), calls=%async_computation | async-start | bytes 16777216 | tf_op jit(solution)/shard_map/all_to_all | solution.py:16
  22.1 0.1 reshape.33
  22.2 146.0 %all-to-all-done = bf16[16,512,512]{2,1,0:T(8,128)(2,1)} async-done(((bf16[16,512,512]{2,1,0:T(8,128)(2,1)}), bf16[16,512,512]{2,1,0:T(8,128)(2,1)}, u32[]{:S(2)}, u32[]{:S(2)}) %all-to-all-start) | async-done | bytes 8388640 | tf_op jit(solution)/shard_map/all_to_all | solution.py:16
  168.2 12.3 %copy.21 = bf16[16,512,512]{1,2,0:T(8,128)(2,1)} copy(bf16[16,512,512]{2,1,0:T(8,128)(2,1)} %all-to-all-done) | data formatting | bytes 16777216 | tf_op jit(solution)/shard_map/all_to_all | solution.py:16
  180.5 12.0 %copy.23 = bf16[512,64,128]{2,1,0:T(8,128)(2,1)} copy(bf16[512,64,128]{0,2,1:T(8,128)(2,1)} %bitcast.54) | data formatting | bytes 16777216
  192.6 213.9 %while.12 = (s32[]{:T(128)}, f32[64,512,128]{2,0,1:T(8,128)}, s32[5,64,2]{1,0,2:T(8,128)S(1)}, bf16[512,64,128]{2,1,0:T(8,128)(2,1)}, bf16[5,64,128,128]{3,2,1,0:T(8,128)(2,1)}, /*index=5*/s32[]{:T(128)}, s32[]{:T(128)}) while((s32[]{:T(128)}, f32[64,512,128]{2,0,1:T(8,128)}, s32[5,64,2]{1,0,2:T(8,128)S(1)}, ...), condition=%wide.region_1.2_spmd.clone.clone, body=%wide.region_0.1_spmd.clone.clone.sunk | while | flops 4844429312 | bytes 94374496 | solution.py:40
  192.6 5.8 convolution_convert_fusion.2
  198.3 14.0 %fusion.35 = f32[64,512,128]{2,1,0:T(8,128)} fusion(bf16[64,512,128]{2,0,1:T(8,128)(2,1)S(1)} %convolution_convert_fusion.2, bf16[5,64,128,128]{3,2,1,0:T(8,128)(2,1)} %get-tuple-element.157, s32[]{:T(128)S(6)} %copy.41), kind=kOutput, calls=%fused_computation.4.clone.1 | convolution fusion | flops 1073741824 | bytes 27262980 | tf_op jit(solution)/shard_map/while/body/eval_jaxpr/jpc,jcd->jpd/dot_general | solution.py:33
  212.3 20.4 %select_add_fusion.2 = f32[64,512,128]{2,0,1:T(8,128)} fusion(f32[64,512,128]{2,0,1:T(8,128)} %get-tuple-element.147, f32[64,512,128]{2,1,0:T(8,128)} %fusion.35, pred[]{:T(512)S(6)} %compare.3, s32[64]{0:T(128)S(1)} %get-tuple-element.138), kind=kOutput, calls=%fused_computation.3.clone.1 | convolution fusion | flops 3229618176 | bytes 50331904 | tf_op jit(solution)/shard_map/while/body/eval_jaxpr/jv,jpd->vpd/dot_general | solution.py:34
  232.7 5.8 convolution_convert_fusion.2
  238.5 14.0 %fusion.35 = f32[64,512,128]{2,1,0:T(8,128)} fusion(bf16[64,512,128]{2,0,1:T(8,128)(2,1)S(1)} %convolution_convert_fusion.2, bf16[5,64,128,128]{3,2,1,0:T(8,128)(2,1)} %get-tuple-element.157, s32[]{:T(128)S(6)} %copy.41), kind=kOutput, calls=%fused_computation.4.clone.1 | convolution fusion | flops 1073741824 | bytes 27262980 | tf_op jit(solution)/shard_map/while/body/eval_jaxpr/jpc,jcd->jpd/dot_general | solution.py:33
  252.5 23.7 %select_add_fusion.2 = f32[64,512,128]{2,0,1:T(8,128)} fusion(f32[64,512,128]{2,0,1:T(8,128)} %get-tuple-element.147, f32[64,512,128]{2,1,0:T(8,128)} %fusion.35, pred[]{:T(512)S(6)} %compare.3, s32[64]{0:T(128)S(1)} %get-tuple-element.138), kind=kOutput, calls=%fused_computation.3.clone.1 | convolution fusion | flops 3229618176 | bytes 50331904 | tf_op jit(solution)/shard_map/while/body/eval_jaxpr/jv,jpd->vpd/dot_general | solution.py:34
  276.2 5.8 convolution_convert_fusion.2
  281.9 14.0 %fusion.35 = f32[64,512,128]{2,1,0:T(8,128)} fusion(bf16[64,512,128]{2,0,1:T(8,128)(2,1)S(1)} %convolution_convert_fusion.2, bf16[5,64,128,128]{3,2,1,0:T(8,128)(2,1)} %get-tuple-element.157, s32[]{:T(128)S(6)} %copy.41), kind=kOutput, calls=%fused_computation.4.clone.1 | convolution fusion | flops 1073741824 | bytes 27262980 | tf_op jit(solution)/shard_map/while/body/eval_jaxpr/jpc,jcd->jpd/dot_general | solution.py:33
  295.9 23.7 %select_add_fusion.2 = f32[64,512,128]{2,0,1:T(8,128)} fusion(f32[64,512,128]{2,0,1:T(8,128)} %get-tuple-element.147, f32[64,512,128]{2,1,0:T(8,128)} %fusion.35, pred[]{:T(512)S(6)} %compare.3, s32[64]{0:T(128)S(1)} %get-tuple-element.138), kind=kOutput, calls=%fused_computation.3.clone.1 | convolution fusion | flops 3229618176 | bytes 50331904 | tf_op jit(solution)/shard_map/while/body/eval_jaxpr/jv,jpd->vpd/dot_general | solution.py:34
  319.6 5.8 convolution_convert_fusion.2
  325.4 14.0 %fusion.35 = f32[64,512,128]{2,1,0:T(8,128)} fusion(bf16[64,512,128]{2,0,1:T(8,128)(2,1)S(1)} %convolution_convert_fusion.2, bf16[5,64,128,128]{3,2,1,0:T(8,128)(2,1)} %get-tuple-element.157, s32[]{:T(128)S(6)} %copy.41), kind=kOutput, calls=%fused_computation.4.clone.1 | convolution fusion | flops 1073741824 | bytes 27262980 | tf_op jit(solution)/shard_map/while/body/eval_jaxpr/jpc,jcd->jpd/dot_general | solution.py:33
  339.4 23.7 %select_add_fusion.2 = f32[64,512,128]{2,0,1:T(8,128)} fusion(f32[64,512,128]{2,0,1:T(8,128)} %get-tuple-element.147, f32[64,512,128]{2,1,0:T(8,128)} %fusion.35, pred[]{:T(512)S(6)} %compare.3, s32[64]{0:T(128)S(1)} %get-tuple-element.138), kind=kOutput, calls=%fused_computation.3.clone.1 | convolution fusion | flops 3229618176 | bytes 50331904 | tf_op jit(solution)/shard_map/while/body/eval_jaxpr/jv,jpd->vpd/dot_general | solution.py:34
  363.1 5.8 convolution_convert_fusion.2
  368.8 14.0 %fusion.35 = f32[64,512,128]{2,1,0:T(8,128)} fusion(bf16[64,512,128]{2,0,1:T(8,128)(2,1)S(1)} %convolution_convert_fusion.2, bf16[5,64,128,128]{3,2,1,0:T(8,128)(2,1)} %get-tuple-element.157, s32[]{:T(128)S(6)} %copy.41), kind=kOutput, calls=%fused_computation.4.clone.1 | convolution fusion | flops 1073741824 | bytes 27262980 | tf_op jit(solution)/shard_map/while/body/eval_jaxpr/jpc,jcd->jpd/dot_general | solution.py:33
  382.8 23.7 %select_add_fusion.2 = f32[64,512,128]{2,0,1:T(8,128)} fusion(f32[64,512,128]{2,0,1:T(8,128)} %get-tuple-element.147, f32[64,512,128]{2,1,0:T(8,128)} %fusion.35, pred[]{:T(512)S(6)} %compare.3, s32[64]{0:T(128)S(1)} %get-tuple-element.138), kind=kOutput, calls=%fused_computation.3.clone.1 | convolution fusion | flops 3229618176 | bytes 50331904 | tf_op jit(solution)/shard_map/while/body/eval_jaxpr/jv,jpd->vpd/dot_general | solution.py:34
  406.5 0.2 all-gather.2.cloned.1.call-start
  406.7 0.3 all-gather.2.cloned.1.call-update
  407.2 224.3 %all-reduce.2.cloned.1.call-done = f32[64,512,128]{2,0,1:T(8,128)} async-done(((f32[64,512,128]{2,0,1:T(8,128)}), f32[64,512,128]{2,0,1:T(8,128)}) %all-reduce.2.cloned.1.call-update) | async-done | bytes 16777232 | tf_op jit(solution)/shard_map/psum | solution.py:41
  631.5 1.8 dynamic-slice_bitcast_fusion
  633.2 0.4 copy.24
  633.6 5.8 fusion.18
  639.5 1.3 copy.25
  (22 shorter events, 0.3 us)
Async XLA Ops:
  9.2 4.1 copy-start
  13.2 8.9 %copy-start.1 = (s32[320,2]{0,1:T(2,128)S(1)}, s32[320,2]{0,1:T(2,128)}, u32[]{:S(2)}) copy-start(s32[320,2]{0,1:T(2,128)} %param.10) | copy-start | bytes 7684
  13.2 154.9 %all-to-all-start = ((bf16[16,512,512]{2,1,0:T(8,128)(2,1)}), bf16[16,512,512]{2,1,0:T(8,128)(2,1)}, u32[]{:S(2)}, u32[]{:S(2)}) async-start(bf16[16,512,512]{2,1,0:T(8,128)(2,1)} %stack.3), calls=%async_computation | async-start | bytes 16777216 | tf_op jit(solution)/shard_map/all_to_all | solution.py:16
  22.0 609.4 %all-reduce.2.cloned.1.call-start = ((), (), s32[]{:S(2)}) async-start(), calls=%async_computation.1 | async-start | bytes 33554432 | tf_op jit(solution)/shard_map/psum | solution.py:41
  406.5 0.7 copy-start.2
  406.5 227.1 %all-gather.2.cloned.1.call-start = ((), (), s32[]{:S(2)}) async-start(), calls=%async_computation.2 | async-start | bytes 4718592 | tf_op jit(solution)/shard_map/all_gather | solution.py:46
Sparse Core Ops, SparseCore 0:
  406.6 224.8 all-reduce.1
Sparse Core Ops, SparseCore 1:
  408.7 36.8 all-gather.1
